TPU v7x, 32 devices: a whole 2x2x4 slice. The times are simulated.
32 devices in a mesh: region: 8 (over z, y), lev: 4 (over x, core).
Axes of the slice: x: 2, y: 2, z: 4, core: 2. Of those that a mesh axis runs over, the one named last changes fastest.
Arguments:
- background_members: bfloat16 [80, 16, 1024, 8], P(None, 'lev', 'region'), may hold values from -6 to 6
- channel_height_kernel: float32 [8, 16], P(None, 'lev'), may hold values from -1.5 to 1.5
- sensor_spread_down: float32 [4], replicated, may hold values from 0.2 to 0.6
- sensor_spread_across: float32 [4], replicated, may hold values from 0.2 to 0.6
- measurement_placement: int32 [4, 64], replicated, may hold values from 0 to 511
- measurement_ordering: int32 [4, 64], replicated, may hold values from 0 to 63, each once within a row
- group_area_number: int32 [4], replicated, may hold values from 0 to 7
- taper_radius_limit: int32 [8], replicated, may hold values from 8 to 16
- measured_amounts: float32 [4, 64], replicated, may hold values from -8 to 8
- measurement_noise_spread: float32 [4, 64], replicated, may hold values from 0.05 to 0.5
Outputs:
- analysis: bfloat16 [80, 16, 8, 1024], P(None, 'lev', 'region')
All inputs are finite; a program needn't handle non-finite values.
Results may differ from a plain program's by a relative error of at most 0.001.
Values may be sent and summed in bfloat16 or wider, within the bound.
No kernel may reach another device: no remote copies, remote signals or barrier semaphores. Data moves between devices by JAX's collectives and lax.ppermute only.
A program may use at most 128 MiB of HBM per device.

v0:
```python
import jax
import jax.numpy as jnp
from jax import lax
from jax.sharding import PartitionSpec as P

TILE = 32
STRIDE = 4
highest = lax.Precision.HIGHEST
group_width = 32


def footprint(present_state_grid, sensor_spread_down, sensor_spread_across, channel_height_kernel):
    members, levels, pixels = present_state_grid.shape
    foot_cells = TILE // STRIDE
    tiles_view = present_state_grid.reshape(members, levels, foot_cells, STRIDE, foot_cells, STRIDE)
    blocks = jnp.einsum(
        "klaicj,i,j->klac", tiles_view, sensor_spread_down, sensor_spread_across, precision=highest
    )
    blocks = blocks.reshape(members, levels, foot_cells * foot_cells)
    weighted = jnp.einsum("klq,hl->khq", blocks, channel_height_kernel, precision=highest)
    return weighted.reshape(members, -1)


def taper_weight(distance, cut_radius):
    return jnp.maximum(0.0, 1.0 - distance / (cut_radius + 1.0))


def serial_block(current, values, errors):
    denominator = current.shape[0] - 1.0
    recorded = []
    for column_id in range(current.shape[1]):
        column = current[:, column_id]
        center_col = jnp.mean(column)
        anomaly_col = column - center_col
        variance = jnp.sum(anomaly_col * anomaly_col) / denominator + errors[column_id]
        alpha_gain = 1.0 / (1.0 + jnp.sqrt(errors[column_id] / variance))
        innovation = values[column_id] - center_col
        recorded.append(column)
        anomaly_all = current - jnp.mean(current, axis=0, keepdims=True)
        covariance = jnp.dot(anomaly_col, anomaly_all, precision=highest) / denominator
        current = current + jnp.outer(innovation - alpha_gain * anomaly_col, covariance / variance)
    return jnp.stack(recorded, axis=1)


def block_terms(recorded, values, errors):
    denominator = recorded.shape[0] - 1.0
    center_blk = jnp.mean(recorded, axis=0)
    anomaly_rec = recorded - center_blk[None]
    variance = jnp.sum(anomaly_rec * anomaly_rec, axis=0) / denominator + errors
    alpha_gain = 1.0 / (1.0 + jnp.sqrt(errors / variance))
    scale_pert = alpha_gain / (denominator * variance)
    scale_mean = (values - center_blk) / (denominator * variance)
    return (anomaly_rec, scale_pert, scale_mean)


def advance(transforms, offsets, anomaly_rec, scale_pert, scale_mean, tapers):
    block_size = anomaly_rec.shape[1]
    gram_matrix = jnp.dot(anomaly_rec.T, anomaly_rec, precision=highest)
    upper_part = jnp.triu(gram_matrix, 1)
    coef_pert = tapers * scale_pert[None]
    coef_mean = tapers * scale_mean[None]
    identity_blk = jnp.eye(block_size, dtype=jnp.float32)[None]
    nilpotent = coef_pert[:, :, None] * upper_part[None]
    inverse = identity_blk - nilpotent
    power = nilpotent
    for level_id in range((block_size - 1).bit_length() - 1):
        power = jnp.einsum("tij,tjk->tik", power, power, precision=highest)
        inverse = inverse + jnp.einsum("tij,tjk->tik", inverse, power, precision=highest)
    factor = inverse * coef_pert[:, None, :]
    carried = jnp.einsum("ij,tj->ti", upper_part, coef_mean, precision=highest)
    weights_mean = coef_mean - jnp.einsum("tij,tj->ti", factor, carried, precision=highest)
    mapped = jnp.einsum("tkm,mj->tkj", transforms, anomaly_rec, precision=highest)
    offsets = offsets + jnp.einsum("tkj,tj->tk", mapped, weights_mean, precision=highest)
    folded = jnp.einsum("tkj,tjl->tkl", mapped, factor, precision=highest)
    transforms = transforms - jnp.einsum("tkl,ml->tkm", folded, anomaly_rec, precision=highest)
    return (transforms, offsets)


def run_batch(base_priors, values, errors, transforms, offsets, tapers, target):
    center = jnp.mean(base_priors, axis=0)
    anomaly = base_priors - center[None]
    count_blocks = base_priors.shape[1] // group_width

    def one_block(block_id, state_carry):
        transforms, offsets, recorded_all = state_carry
        start = block_id * group_width
        anomaly_blk = lax.dynamic_slice_in_dim(anomaly, start, group_width, 1)
        center_blk = lax.dynamic_slice_in_dim(center, start, group_width, 0)
        values_blk = lax.dynamic_slice_in_dim(values, start, group_width, 0)
        errors_blk = lax.dynamic_slice_in_dim(errors, start, group_width, 0)
        tapers_blk = lax.dynamic_slice_in_dim(tapers, start, group_width, 1)
        current = (
            jnp.dot(transforms[target].T, anomaly_blk, precision=highest)
            + (center_blk + jnp.dot(offsets[target], anomaly_blk, precision=highest))[None]
        )
        recorded = serial_block(current, values_blk, errors_blk)
        anomaly_rec, scale_pert, scale_mean = block_terms(recorded, values_blk, errors_blk)
        transforms, offsets = advance(
            transforms, offsets, anomaly_rec, scale_pert, scale_mean, tapers_blk
        )
        recorded_all = lax.dynamic_update_slice_in_dim(recorded_all, recorded, start, 1)
        return (transforms, offsets, recorded_all)

    return lax.fori_loop(
        0, count_blocks, one_block, (transforms, offsets, jnp.zeros_like(base_priors))
    )


def body(
    background_members,
    channel_height_kernel,
    sensor_spread_down,
    sensor_spread_across,
    measurement_placement,
    measurement_ordering,
    group_area_number,
    taper_radius_limit,
    measured_amounts,
    measurement_noise_spread,
):
    own_region = lax.axis_index("region")
    present_state_grid = lax.all_to_all(
        background_members, "region", split_axis=3, concat_axis=2, tiled=True
    )[:, :, :, 0].astype(jnp.float32)
    present_state_grid, partial_priors = (
        present_state_grid,
        footprint(
            present_state_grid, sensor_spread_down, sensor_spread_across, channel_height_kernel
        ),
    )
    priors = lax.psum(partial_priors, "lev")
    members, levels, pixels = present_state_grid.shape
    flat_field = present_state_grid.reshape(members, levels * pixels)
    center = jnp.mean(flat_field, axis=0)
    anomaly = flat_field - center[None]
    picked = jnp.take_along_axis(measurement_placement, measurement_ordering, axis=1)
    values_all = jnp.take_along_axis(measured_amounts, measurement_ordering, axis=1)
    errors_all = jnp.take_along_axis(measurement_noise_spread, measurement_ordering, axis=1)
    foot_cells = TILE // STRIDE * (TILE // STRIDE)
    channels = picked // foot_cells
    channel_ids = jnp.arange(taper_radius_limit.shape[0], dtype=jnp.int32)
    cut_radius = jnp.sum(
        jnp.where(channels[:, :, None] == channel_ids, taper_radius_limit, 0), axis=2
    ).astype(jnp.float32)
    batches = measurement_placement.shape[0]
    eye_members = jnp.eye(members, dtype=jnp.float32)
    hosting = own_region == group_area_number
    chosen = jnp.take(priors, picked.reshape(-1), axis=1).reshape(members, batches, -1)
    chosen = jnp.where(hosting[None, :, None], chosen, 0.0)
    bases = lax.psum(chosen, "region")
    targets = jnp.concatenate([own_region[None], group_area_number])
    count_targets = batches + 1
    transforms = jnp.tile(eye_members[None], (count_targets, 1, 1))
    offsets = jnp.zeros((count_targets, members), jnp.float32)
    for batch_id in range(batches):
        distance = jnp.abs(targets - group_area_number[batch_id]).astype(jnp.float32)
        tapers = taper_weight(distance[:, None], cut_radius[batch_id][None])
        outcome = run_batch(
            bases[:, batch_id],
            values_all[batch_id],
            errors_all[batch_id],
            transforms,
            offsets,
            tapers,
            1 + batch_id,
        )
        transforms, offsets = (outcome[0], outcome[1])
    mixing = transforms[0] + offsets[0][:, None]
    result = jnp.dot(mixing.T, anomaly, precision=highest) + center[None]
    return result.reshape(members, levels, 1, pixels).astype(jnp.bfloat16)


def solution(mesh):
    return jax.shard_map(
        body,
        mesh=mesh,
        in_specs=(
            P(None, "lev", "region", None),
            P(None, "lev"),
            P(),
            P(),
            P(),
            P(),
            P(),
            P(),
            P(),
            P(),
        ),
        out_specs=P(None, "lev", "region", None),
        check_vma=False,
    )
```

profile of v0, /device:TPU:0, one launch (start us, length us, event | category | flops | bytes accessed | tf_op | source)
XLA Modules:
  0.0 1444.8 jit_solution(3757707560450293175)
XLA Ops:
  6.5 2.2 copy.48
  8.8 7.5 all-to-all-start
  16.4 2.4 gather_fusion.1
  20.6 1.8 abs_convert_fusion.1
  22.5 2.4 gather_fusion.3
  25.1 2.4 gather_fusion.2
  27.8 5.8 all-to-all-done
  34.9 0.9 multiply_reduce_fusion.4
  36.2 0.8 copy.84
  37.4 31.1 %all-reduce.3.cloned.1.call-done = f32[80,512]{0,1:T(8,128)} async-done(((f32[80,512]{0,1:T(8,128)}), f32[80,512]{0,1:T(8,128)}) %all-reduce.3.cloned.1.call-update) | async-done | bytes 163856 | tf_op jit(solution)/shard_map/psum | solution.py:131
  68.5 1.7 gather_fusion
  70.2 0.7 select_select_fusion
  71.8 1.8 copy.54
  73.6 1.5 sub.8074
  75.1 66.7 %all-reduce.5.cloned.1.call-done = f32[80,4,64]{2,0,1:T(8,128)} async-done(((f32[80,4,64]{2,0,1:T(8,128)}), f32[80,4,64]{2,0,1:T(8,128)}) %all-reduce.5.cloned.1.call-update) | async-done | bytes 81936 | tf_op jit(solution)/shard_map/psum | solution.py:150
  141.8 0.9 slice_reduce_fusion.124
  142.7 0.9 bitcast_subtract_fusion.4
  143.6 322.7 %while.64 = (s32[]{:T(128)}, f32[5,80,80]{2,1,0:T(8,128)S(1)}, f32[5,80]{1,0:T(8,128)S(1)}, f32[80,64]{1,0:T(8,128)S(1)}, f32[64]{0:T(128)S(1)}, /*index=5*/f32[...) while((s32[]{:T(128)}, f32[5,80,80]{2,1,0:T(8,128)S(1)}, ...), condition=%wide.region_100.102_spmd.clone, body=%wide.region_4.101_spmd.clone.sunk | while | flops 50354160 | bytes 2541750 | solution.py:104
  145.4 0.7 fusion.2414
  146.1 0.7 fusion.2418
  306.7 0.7 fusion.2414
  466.3 323.2 %while.61 = (s32[]{:T(128)}, f32[5,80,80]{2,1,0:T(8,128)S(1)}, f32[5,80]{1,0:T(8,128)S(1)}, f32[80,64]{1,0:T(8,128)S(1)}, f32[64]{0:T(128)S(1)}, /*index=5*/f32[...) while((s32[]{:T(128)}, f32[5,80,80]{2,1,0:T(8,128)S(1)}, ...), condition=%wide.region_198.200_spmd, body=%wide.region_102.199_spmd.sunk | while | flops 50353360 | bytes 2538531 | solution.py:104
  468.6 0.7 fusion.1910
  629.9 0.7 fusion.1910
  789.5 322.8 %while.62 = (s32[]{:T(128)}, f32[5,80,80]{2,1,0:T(8,128)S(1)}, f32[5,80]{1,0:T(8,128)S(1)}, f32[80,64]{1,0:T(8,128)S(1)}, f32[64]{0:T(128)S(1)}, /*index=5*/f32[...) while((s32[]{:T(128)}, f32[5,80,80]{2,1,0:T(8,128)S(1)}, ...), condition=%wide.region_296.298_spmd, body=%wide.region_200.297_spmd.sunk | while | flops 50353360 | bytes 2538531 | solution.py:104
  791.4 0.7 fusion.2078
  952.7 0.7 fusion.2078
  1112.3 322.9 %while.63 = (s32[]{:T(128)}, f32[5,80,80]{2,1,0:T(8,128)S(1)}, f32[5,80]{1,0:T(8,128)S(1)}, f32[80,64]{1,0:T(8,128)S(1)}, f32[64]{0:T(128)S(1)}, /*index=5*/f32[...) while((s32[]{:T(128)}, f32[5,80,80]{2,1,0:T(8,128)S(1)}, ...), condition=%wide.region_394.396_spmd, body=%wide.region_298.395_spmd.sunk | while | flops 50353360 | bytes 2538531 | solution.py:104
  1114.3 0.7 fusion.2246
  1275.6 0.7 fusion.2246
  1435.1 1.3 fusion.888
  1436.5 1.3 convert_element_type.110
  (1802 shorter events, 480.0 us)
Async XLA Ops:
  6.5 29.2 %copy-start = (f32[8,4]{0,1:T(4,128)S(1)}, f32[8,4]{0,1:T(4,128)}, u32[]{:S(2)}) copy-start(f32[8,4]{0,1:T(4,128)} %param.21) | copy-start | bytes 388
  6.5 9.8 copy-start.5
  6.5 9.9 copy-start.1
  8.8 10.3 copy-start.4
  8.8 11.0 copy-start.7
  8.8 11.0 copy-start.8
  8.8 11.7 copy-start.6
  8.8 13.8 copy-start.2
  8.8 24.7 %all-to-all-start = ((bf16[80,4,128,8]{2,0,1,3:T(8,128)(2,1)}), bf16[80,4,128,8]{2,0,1,3:T(8,128)(2,1)S(1)}, u32[]{:S(2)}, u32[]{:S(2)}) async-start(bf16[80,4,128,8]{2,0,1,3:T(8,128)(2,1)} %copy.48), calls=%async_computation | async-start | bytes 1310720 | tf_op jit(solution)/shard_map/all_to_all | solution.py:122
  16.2 52.2 %all-reduce.3.cloned.1.call-start = ((), (), s32[]{:S(2)}) async-start(), calls=%async_computation.1 | async-start | bytes 524288 | tf_op jit(solution)/shard_map/psum | solution.py:131
  16.4 8.7 copy-start.3
  37.0 104.8 %all-reduce.5.cloned.1.call-start = ((), (), s32[]{:S(2)}) async-start(), calls=%async_computation.2 | async-start | bytes 327680 | tf_op jit(solution)/shard_map/psum | solution.py:150
Sparse Core Ops, SparseCore 0:
  37.1 31.3 all-reduce.2
  71.8 69.9 all-reduce.4
where the time goes:
time: 1460 us; the launch traced here: 1440 us
  loops' own time  810 us (55%)
  other arithmetic  372 us (25%)
  waiting for transfers between devices  104 us (7%)
  matrix products  88.7 us (6%)
  local copies, waits for them, and re-layouts  48.2 us (3%)
    another operation x4, loops' own time, run_batch(): lax.fori_loop(0, count_blocks, one_block, (transforms, offsets, jnp.zeros...  810 us
    reduce_sum x248, other arithmetic, serial_block(): center_col = jnp.mean(column)  154 us
    reduce_sum x248, other arithmetic, serial_block(): jnp.sum(anomaly_col * anomaly_col) / denominator + errors[column_id]  153 us
    psum x1, waiting for transfers between devices, body(): bases = lax.psum(chosen, 'region')  66.7 us
    dot_general x248, matrix products, serial_block(): jnp.dot(anomaly_col, anomaly_all, precision=highest) / denominator  49.4 us
    reduce_sum x240, other arithmetic, serial_block(): anomaly_all = current - jnp.mean(current, axis=0, keepdims=True)  43.3 us
    psum x1, waiting for transfers between devices, body(): priors = lax.psum(partial_priors, 'lev')  31.1 us
  transfers between devices with their start and end apart: 3, of which 3 were waited for; matrix products, arithmetic and copies ran while one was open for 1% of the time, Pallas kernels for 0%

commit v1 on v0

--- a/solution.py
+++ b/solution.py
@@ -147,7 +147,8 @@
     hosting = own_region == group_area_number
     chosen = jnp.take(priors, picked.reshape(-1), axis=1).reshape(members, batches, -1)
     chosen = jnp.where(hosting[None, :, None], chosen, 0.0)
-    bases = lax.psum(chosen, "region")
+    pieces = lax.all_gather(chosen, "region")
+    bases = jnp.sum(pieces, axis=0)
     targets = jnp.concatenate([own_region[None], group_area_number])
     count_targets = batches + 1
     transforms = jnp.tile(eye_members[None], (count_targets, 1, 1))

time: 1460 us -> 1420 us (0.973)
  waiting for transfers between devices: 104 us -> 33.1 us
  blocking collectives: 0 us -> 34 us
    psum x1 -> x0, waiting for transfers between devices: 66.7 us -> none  [body(): bases = lax.psum(chosen, 'region')]
    all_gather x0 -> x1, blocking collectives: none -> 34 us  [body(): pieces = lax.all_gather(chosen, 'region')]
  transfers between devices with their start and end apart: 3 -> 2, of which waited for: 3 -> 2; matrix products, arithmetic and copies ran while one was open for 1% -> 1% of each run, Pallas kernels for 0% -> 0%
where the time goes in v1:
time: 1420 us; the launch traced here: 1400 us
  loops' own time  810 us (57%)
  other arithmetic  370 us (26%)
  matrix products  86.6 us (6%)
  local copies, waits for them, and re-layouts  48.4 us (3%)
  blocking collectives  34 us (2%)
  waiting for transfers between devices  33.1 us (2%)
    another operation x4, loops' own time, run_batch(): lax.fori_loop(0, count_blocks, one_block, (transforms, offsets, jnp.zeros...  810 us
    reduce_sum x248, other arithmetic, serial_block(): center_col = jnp.mean(column)  154 us
    reduce_sum x248, other arithmetic, serial_block(): jnp.sum(anomaly_col * anomaly_col) / denominator + errors[column_id]  153 us
    dot_general x248, matrix products, serial_block(): jnp.dot(anomaly_col, anomaly_all, precision=highest) / denominator  49.4 us
    reduce_sum x240, other arithmetic, serial_block(): anomaly_all = current - jnp.mean(current, axis=0, keepdims=True)  43.3 us
    all_gather x1, blocking collectives, body(): pieces = lax.all_gather(chosen, 'region')  34 us
  transfers between devices with their start and end apart: 2, of which 2 were waited for; matrix products, arithmetic and copies ran while one was open for 1% of the time, Pallas kernels for 0%

profile of v1, /device:TPU:0, one launch (start us, length us, event | category | flops | bytes accessed | tf_op | source)
XLA Modules:
  0.0 1404.2 jit_solution(8630704788993952812)
XLA Ops:
  6.5 2.2 copy.48
  8.8 7.5 all-to-all-start
  16.4 2.4 gather_fusion.1
  20.6 1.8 abs_convert_fusion.1
  22.5 2.4 gather_fusion.3
  25.1 2.4 gather_fusion.2
  27.8 5.8 all-to-all-done
  34.9 0.9 multiply_reduce_fusion.4
  36.2 0.8 copy.87
  37.8 1.8 copy.57
  39.6 1.5 sub.8074
  41.1 27.4 %all-reduce.2.cloned.1.call-done = f32[80,512]{0,1:T(8,128)} async-done(((f32[80,512]{0,1:T(8,128)}), f32[80,512]{0,1:T(8,128)}) %all-reduce.2.cloned.1.call-update) | async-done | bytes 163856 | tf_op jit(solution)/shard_map/psum | solution.py:131
  68.5 1.7 gather_fusion
  70.3 34.0 %all_gather.4 = f32[8,80,4,64]{1,3,2,0:T(8,128)S(1)} all-gather(f32[1,80,4,64]{1,3,2,0:T(8,128)S(1)} %select_select_fusion), channel_id=1, replica_groups=mesh['region'=8,'lev'=4] {'region'}, dimensions={0}, use_global_device_ids=true | all-gather | bytes 737280 | tf_op jit(solution)/shard_map/all_gather | solution.py:150
  104.7 322.2 %while.64 = (s32[]{:T(128)}, f32[5,80,80]{2,1,0:T(8,128)S(1)}, f32[5,80]{1,0:T(8,128)S(1)}, f32[80,64]{0,1:T(8,128)S(1)}, f32[64]{0:T(128)S(1)}, /*index=5*/f32[...) while((s32[]{:T(128)}, f32[5,80,80]{2,1,0:T(8,128)S(1)}, ...), condition=%wide.region_100.102_spmd.clone, body=%wide.region_4.101_spmd.clone.sunk | while | flops 50354160 | bytes 2492598 | solution.py:104
  105.0 0.7 fusion.2380
  266.1 0.7 fusion.2380
  267.5 0.7 fusion.2414
  426.9 322.7 %while.61 = (s32[]{:T(128)}, f32[5,80,80]{2,1,0:T(8,128)S(1)}, f32[5,80]{1,0:T(8,128)S(1)}, f32[80,64]{0,1:T(8,128)S(1)}, f32[64]{0:T(128)S(1)}, /*index=5*/f32[...) while((s32[]{:T(128)}, f32[5,80,80]{2,1,0:T(8,128)S(1)}, ...), condition=%wide.region_198.200_spmd, body=%wide.region_102.199_spmd.sunk | while | flops 50353360 | bytes 2489379 | solution.py:104
  427.7 0.7 fusion.1876
  588.8 0.7 fusion.1876
  590.2 0.7 fusion.1910
  749.7 322.4 %while.62 = (s32[]{:T(128)}, f32[5,80,80]{2,1,0:T(8,128)S(1)}, f32[5,80]{1,0:T(8,128)S(1)}, f32[80,64]{0,1:T(8,128)S(1)}, f32[64]{0:T(128)S(1)}, /*index=5*/f32[...) while((s32[]{:T(128)}, f32[5,80,80]{2,1,0:T(8,128)S(1)}, ...), condition=%wide.region_296.298_spmd, body=%wide.region_200.297_spmd.sunk | while | flops 50353360 | bytes 2489379 | solution.py:104
  750.1 0.7 fusion.2044
  751.5 0.7 fusion.2078
  911.2 0.7 fusion.2044
  912.6 0.7 fusion.2078
  1072.0 322.4 %while.63 = (s32[]{:T(128)}, f32[5,80,80]{2,1,0:T(8,128)S(1)}, f32[5,80]{1,0:T(8,128)S(1)}, f32[80,64]{0,1:T(8,128)S(1)}, f32[64]{0:T(128)S(1)}, /*index=5*/f32[...) while((s32[]{:T(128)}, f32[5,80,80]{2,1,0:T(8,128)S(1)}, ...), condition=%wide.region_394.396_spmd, body=%wide.region_298.395_spmd.sunk | while | flops 50353360 | bytes 2489379 | solution.py:104
  1072.5 0.7 fusion.2212
  1233.6 0.7 fusion.2212
  1394.5 1.3 fusion.888
  1395.8 1.3 convert_element_type.110
  (1800 shorter events, 476.0 us)
Async XLA Ops:
  6.5 29.2 %copy-start = (f32[8,4]{0,1:T(4,128)S(1)}, f32[8,4]{0,1:T(4,128)}, u32[]{:S(2)}) copy-start(f32[8,4]{0,1:T(4,128)} %param.21) | copy-start | bytes 388
  6.5 9.8 copy-start.5
  6.5 9.9 copy-start.1
  8.8 10.3 copy-start.4
  8.8 11.0 copy-start.7
  8.8 11.0 copy-start.8
  8.8 11.7 copy-start.6
  8.8 13.8 copy-start.2
  8.8 24.7 %all-to-all-start = ((bf16[80,4,128,8]{2,0,1,3:T(8,128)(2,1)}), bf16[80,4,128,8]{2,0,1,3:T(8,128)(2,1)S(1)}, u32[]{:S(2)}, u32[]{:S(2)}) async-start(bf16[80,4,128,8]{2,0,1,3:T(8,128)(2,1)} %copy.48), calls=%async_computation | async-start | bytes 1310720 | tf_op jit(solution)/shard_map/all_to_all | solution.py:122
  16.2 52.2 %all-reduce.2.cloned.1.call-start = ((), (), s32[]{:S(2)}) async-start(), calls=%async_computation.1 | async-start | bytes 524288 | tf_op jit(solution)/shard_map/psum | solution.py:131
  16.4 8.7 copy-start.3
Sparse Core Ops, SparseCore 0:
  37.1 31.3 all-reduce.1
